TPU v7x, 32 devices: a whole 2x2x4 slice. The times are simulated.
32 devices in a mesh: dp: 2 (over y), gx: 4 (over z), gy: 4 (over x, core).
Axes of the slice: x: 2, y: 2, z: 4, core: 2. Of those that a mesh axis runs over, the one named last changes fastest.
Arguments:
- block_input: bfloat16 [3, 2, 2048, 1280], P(None, 'dp', ('gx', 'gy')), may hold values from -6 to 6
- picture: int32 [3, 2, 2048], P(None, 'dp'), may hold values from 0 to 24, as said below
- position: int32 [2, 3, 2, 2048], P(None, None, 'dp'), may hold values from 0 to 31, as said below
- patch_mask: int32 [3, 2, 2048], P(None, 'dp'), may hold values from 0 to 1, as said below
- gain_attn: float32 [1280], replicated, may hold values from 0.5 to 1.5
- shift_attn: float32 [1280], replicated, may hold values from -3 to 3
- w_query: bfloat16 [1280, 1280], P(('dp', 'gx'), 'gy'), may hold values from -0.15625 to 0.15625
- b_query: float32 [1280], replicated, may hold values from -3 to 3
- w_key: bfloat16 [1280, 1280], P(('dp', 'gx'), 'gy'), may hold values from -0.15625 to 0.15625
- b_key: float32 [1280], replicated, may hold values from -3 to 3
- w_value: bfloat16 [1280, 1280], P(('dp', 'gx'), 'gy'), may hold values from -0.15625 to 0.15625
- b_value: float32 [1280], replicated, may hold values from -3 to 3
- w_out: bfloat16 [1280, 1280], P(('dp', 'gx'), 'gy'), may hold values from -1.25 to 1.25
- b_out: float32 [1280], replicated, may hold values from -3 to 3
- gain_mlp: float32 [1280], replicated, may hold values from 0.5 to 1.5
- shift_mlp: float32 [1280], replicated, may hold values from -3 to 3
- w_up: bfloat16 [1280, 5120], P(('dp', 'gx'), 'gy'), may hold values from -0.15625 to 0.15625
- b_up: float32 [5120], replicated, may hold values from -3 to 3
- w_down: bfloat16 [1280, 5120], P(('dp', 'gx'), 'gy'), may hold values from -0.15625 to 0.15625
- b_down: float32 [1280], replicated, may hold values from -3 to 3
- out_grad: bfloat16 [3, 2, 2048, 1280], P(None, 'dp', ('gx', 'gy')), may hold values from -6 to 6
Outputs:
- block_output: bfloat16 [3, 2, 2048, 1280], P(None, 'dp', ('gx', 'gy'))
- input_grad: float32 [3, 2, 2048, 1280], P(None, 'dp', ('gx', 'gy'))
- gain_attn_grad: float32 [1280], replicated
- shift_attn_grad: float32 [1280], replicated
- w_query_grad: float32 [1280, 1280], P(('dp', 'gx'), 'gy')
- b_query_grad: float32 [1280], replicated
- w_key_grad: float32 [1280, 1280], P(('dp', 'gx'), 'gy')
- b_key_grad: float32 [1280], replicated
- w_value_grad: float32 [1280, 1280], P(('dp', 'gx'), 'gy')
- b_value_grad: float32 [1280], replicated
- w_out_grad: float32 [1280, 1280], P(('dp', 'gx'), 'gy')
- b_out_grad: float32 [1280], replicated
- gain_mlp_grad: float32 [1280], replicated
- shift_mlp_grad: float32 [1280], replicated
- w_up_grad: float32 [1280, 5120], P(('dp', 'gx'), 'gy')
- b_up_grad: float32 [5120], replicated
- w_down_grad: float32 [1280, 5120], P(('dp', 'gx'), 'gy')
- b_down_grad: float32 [1280], replicated
Inputs may be any that keep to these rules, and one draw needn't show every extreme that they name: Each row holds whole pictures one after another from slot 0, numbered 0, 1, 2, ... in that order; every picture has h by w patches, one of each row 32 by 32 and the others with sides from 10 to 31; the slots after the last picture, at least one a row, hold 24. position[0] and position[1] are the row and column of a patch within its picture, in row-major order; padding slots hold 0. `patch_mask`: 1 on the slots of pictures, 0 on the padding after them.
All inputs are finite; a program needn't handle non-finite values.
Results may differ from a plain program's by a relative error of at most 0.02.
Values may be sent and summed in bfloat16 or wider, within the bound.
No kernel may reach another device: no remote copies, remote signals or barrier semaphores. Data moves between devices by JAX's collectives and lax.ppermute only.
A program may use at most 144 MiB of HBM per device.

v0:
```python
import jax
import jax.numpy as jnp
from jax import lax
from jax.sharding import PartitionSpec as P

HEAD_DIM = 80
EPSILON = 1e-06


def layer_norm(values, norm_gain, norm_shift):
    center = values - jnp.mean(values, axis=-1, keepdims=True)
    factor = lax.rsqrt(jnp.mean(center * center, axis=-1, keepdims=True) + EPSILON)
    normal = center * factor
    return (normal * norm_gain + norm_shift, normal, factor)


def norm_back(upstream, normal, factor, norm_gain):
    shaped = upstream * norm_gain
    first_mean = jnp.mean(shaped, axis=-1, keepdims=True)
    second_mean = jnp.mean(shaped * normal, axis=-1, keepdims=True)
    return factor * (shaped - first_mean - normal * second_mean)


def rotary_tables(position_rows, first_slot, slot_total):
    quarter = HEAD_DIM // 4
    inverse = 10000.0 ** (-jnp.arange(quarter, dtype=jnp.float32) / quarter)
    picked = lax.dynamic_slice_in_dim(position_rows, first_slot, slot_total, 2).astype(jnp.float32)
    along_rows = jnp.transpose(picked[0])[:, :, None] * inverse
    along_cols = jnp.transpose(picked[1])[:, :, None] * inverse
    angles = jnp.concatenate([along_rows, along_cols, along_rows, along_cols], axis=-1)[
        :, :, None, :
    ]
    return (jnp.cos(angles), jnp.sin(angles))


def rotate(values, cos_table, sin_table):
    halfway = HEAD_DIM // 2
    turned = jnp.concatenate([-values[..., halfway:], values[..., :halfway]], axis=-1)
    return values * cos_table + turned * sin_table


def rotate_back(upstream, cos_table, sin_table):
    halfway = HEAD_DIM // 2
    moved = upstream * sin_table
    return upstream * cos_table + jnp.concatenate(
        [moved[..., halfway:], -moved[..., :halfway]], axis=-1
    )


def attention_scores(queries, keys_all, visible):
    raw = jnp.einsum(
        "qrhd,krhd->rhqk", queries, keys_all, preferred_element_type=jnp.float32
    ) * HEAD_DIM ** (-0.5)
    return jnp.where(visible[:, None], raw, -1e30)


def per_device(
    block_input,
    picture,
    position,
    patch_mask,
    gain_attn,
    shift_attn,
    w_query,
    b_query,
    w_key,
    b_key,
    w_value,
    b_value,
    w_out,
    b_out,
    gain_mlp,
    shift_mlp,
    w_up,
    b_up,
    w_down,
    b_down,
    out_grad,
):
    across = lax.axis_size("gy")
    column = lax.axis_index("gy")
    segment = lax.axis_index("gx")
    micro_count = block_input.shape[0]
    row_count = block_input.shape[1]
    own_rows = block_input.shape[2]
    slot_count = picture.shape[2]
    query_rows = own_rows * across
    head_cols = w_query.shape[1]
    hidden_cols = w_up.shape[1]
    heads_here = head_cols // HEAD_DIM
    query_start = segment * query_rows
    head_start = column * head_cols
    up_start = column * hidden_cols
    scaling = HEAD_DIM ** (-0.5)
    query_bias = lax.dynamic_slice_in_dim(b_query, head_start, head_cols)
    key_bias = lax.dynamic_slice_in_dim(b_key, head_start, head_cols)
    value_bias = lax.dynamic_slice_in_dim(b_value, head_start, head_cols)
    up_bias = lax.dynamic_slice_in_dim(b_up, up_start, hidden_cols)
    head_shape = (query_rows, row_count, heads_here, HEAD_DIM)
    grad_shards = [
        jnp.zeros(shard.shape, jnp.float32)
        for shard in (w_query, w_key, w_value, w_out, w_up, w_down)
    ]
    sum_gain_attn = jnp.zeros(gain_attn.shape, jnp.float32)
    sum_shift_attn = jnp.zeros(gain_attn.shape, jnp.float32)
    sum_query_bias = jnp.zeros((head_cols,), jnp.float32)
    sum_key_bias = jnp.zeros((head_cols,), jnp.float32)
    sum_value_bias = jnp.zeros((head_cols,), jnp.float32)
    sum_out_bias = jnp.zeros(b_out.shape, jnp.float32)
    sum_gain_mlp = jnp.zeros(gain_mlp.shape, jnp.float32)
    sum_shift_mlp = jnp.zeros(gain_mlp.shape, jnp.float32)
    sum_up_bias = jnp.zeros((hidden_cols,), jnp.float32)
    sum_down_bias = jnp.zeros(b_down.shape, jnp.float32)
    outputs = []
    input_grads = []
    for micro in range(micro_count):
        blocks = (
            lax.all_gather(w_query, ("dp", "gx"), axis=0, tiled=True),
            lax.all_gather(w_key, ("dp", "gx"), axis=0, tiled=True),
            lax.all_gather(w_value, ("dp", "gx"), axis=0, tiled=True),
            lax.all_gather(w_out, ("dp", "gx"), axis=0, tiled=True),
            lax.all_gather(w_up, ("dp", "gx"), axis=0, tiled=True),
            lax.all_gather(w_down, ("dp", "gx"), axis=0, tiled=True),
        )
        full_query, full_key, full_value, full_out, full_up, full_down = blocks
        inputs = jnp.transpose(block_input[micro], (1, 0, 2)).astype(jnp.float32)
        normed, normal_one, factor_one = layer_norm(inputs, gain_attn, shift_attn)
        normed_rows = lax.all_gather(normed.astype(jnp.bfloat16), "gy", axis=0, tiled=True)
        cos_table, sin_table = rotary_tables(position[:, micro], query_start, query_rows)
        query_pre = (
            jnp.einsum("srd,dc->src", normed_rows, full_query, preferred_element_type=jnp.float32)
            + query_bias
        )
        key_pre = (
            jnp.einsum("srd,dc->src", normed_rows, full_key, preferred_element_type=jnp.float32)
            + key_bias
        )
        value_pre = (
            jnp.einsum("srd,dc->src", normed_rows, full_value, preferred_element_type=jnp.float32)
            + value_bias
        )
        queries = rotate(query_pre.reshape(head_shape), cos_table, sin_table).astype(jnp.bfloat16)
        key_here = rotate(key_pre.reshape(head_shape), cos_table, sin_table).astype(jnp.bfloat16)
        value_here = value_pre.reshape(head_shape).astype(jnp.bfloat16)
        keys_all, values_all = (
            lax.all_gather(key_here, "gx", axis=0, tiled=True),
            lax.all_gather(value_here, "gx", axis=0, tiled=True),
        )
        picture_row = picture[micro]
        query_picture = lax.dynamic_slice_in_dim(picture_row, query_start, query_rows, 1)
        query_places = query_start + jnp.arange(query_rows)
        same_picture = (query_picture[:, :, None] == picture_row[:, None, :]) & (
            patch_mask[micro][:, None, :] == 1
        )
        itself = (query_places[:, None] == jnp.arange(slot_count)[None, :])[None]
        visible = same_picture | itself
        scores = attention_scores(queries, keys_all, visible)
        highest = jnp.max(scores, axis=-1, keepdims=True)
        raised = jnp.exp(scores - highest)
        summed = jnp.sum(raised, axis=-1, keepdims=True)
        log_total = highest + jnp.log(summed)
        attend = (raised / summed).astype(jnp.bfloat16)
        mixture = jnp.einsum(
            "rhqk,krhd->qrhd", attend, values_all, preferred_element_type=jnp.float32
        )
        mixture = mixture.reshape(query_rows, row_count, head_cols).astype(jnp.bfloat16)
        branch = (
            lax.psum_scatter(
                jnp.einsum("srh,oh->sro", mixture, full_out, preferred_element_type=jnp.float32),
                "gy",
                scatter_dimension=0,
                tiled=True,
            )
            + b_out
        )
        middle = inputs + branch
        normed_two, normal_two, factor_two = layer_norm(middle, gain_mlp, shift_mlp)
        mlp_rows = lax.all_gather(normed_two.astype(jnp.bfloat16), "gy", axis=0, tiled=True)
        hidden = (
            jnp.einsum("srd,df->srf", mlp_rows, full_up, preferred_element_type=jnp.float32)
            + up_bias
        )
        squashed = jax.nn.sigmoid(1.702 * hidden)
        active = (hidden * squashed).astype(jnp.bfloat16)
        result = (
            lax.psum_scatter(
                jnp.einsum(
                    "srf,of->sro", active, full_down, preferred_element_type=jnp.float32
                ).astype(jnp.bfloat16),
                "gy",
                scatter_dimension=0,
                tiled=True,
            ).astype(jnp.float32)
            + b_down
        )
        outputs.append(jnp.transpose(middle + result, (1, 0, 2)).astype(jnp.bfloat16))
        cotangent = jnp.transpose(out_grad[micro], (1, 0, 2))
        sum_down_bias = sum_down_bias + jnp.sum(cotangent.astype(jnp.float32), axis=(0, 1))
        cot_rows = lax.all_gather(cotangent, "gy", axis=0, tiled=True)
        grad_down = jnp.einsum("srd,srf->df", cot_rows, active, preferred_element_type=jnp.float32)
        active_grad = jnp.einsum(
            "srd,df->srf", cot_rows, full_down, preferred_element_type=jnp.float32
        )
        hidden_grad = (
            active_grad * (squashed + 1.702 * hidden * squashed * (1.0 - squashed))
        ).astype(jnp.bfloat16)
        sum_up_bias = sum_up_bias + jnp.sum(hidden_grad.astype(jnp.float32), axis=(0, 1))
        grad_up = jnp.einsum(
            "srd,srf->df", mlp_rows, hidden_grad, preferred_element_type=jnp.float32
        )
        normed_two_grad = lax.psum_scatter(
            jnp.einsum("srf,df->srd", hidden_grad, full_up, preferred_element_type=jnp.float32),
            "gy",
            scatter_dimension=0,
            tiled=True,
        )
        sum_gain_mlp = sum_gain_mlp + jnp.sum(normed_two_grad * normal_two, axis=(0, 1))
        sum_shift_mlp = sum_shift_mlp + jnp.sum(normed_two_grad, axis=(0, 1))
        middle_grad = cotangent.astype(jnp.float32) + norm_back(
            normed_two_grad, normal_two, factor_two, gain_mlp
        )
        branch_grad = middle_grad.astype(jnp.bfloat16)
        sum_out_bias = sum_out_bias + jnp.sum(branch_grad.astype(jnp.float32), axis=(0, 1))
        branch_rows = lax.all_gather(branch_grad, "gy", axis=0, tiled=True)
        grad_out = jnp.einsum(
            "srd,srh->dh", branch_rows, mixture, preferred_element_type=jnp.float32
        )
        mixture_grad = jnp.einsum(
            "srd,dh->srh", branch_rows, full_out, preferred_element_type=jnp.float32
        )
        mixture_grad = mixture_grad.astype(jnp.bfloat16).reshape(head_shape)
        again = jnp.exp(attention_scores(queries, keys_all, visible) - log_total)
        again_low = again.astype(jnp.bfloat16)
        attend_grad = jnp.einsum(
            "qrhd,krhd->rhqk", mixture_grad, values_all, preferred_element_type=jnp.float32
        )
        score_grad = (
            again * (attend_grad - jnp.sum(again * attend_grad, axis=-1, keepdims=True))
        ).astype(jnp.bfloat16)
        query_grad = (
            jnp.einsum("rhqk,krhd->qrhd", score_grad, keys_all, preferred_element_type=jnp.float32)
            * scaling
        )
        key_part = (
            jnp.einsum("rhqk,qrhd->krhd", score_grad, queries, preferred_element_type=jnp.float32)
            * scaling
        )
        value_part = jnp.einsum(
            "rhqk,qrhd->krhd", again_low, mixture_grad, preferred_element_type=jnp.float32
        )
        key_grad, value_grad = (
            lax.psum_scatter(key_part, "gx", scatter_dimension=0, tiled=True),
            lax.psum_scatter(value_part, "gx", scatter_dimension=0, tiled=True),
        )
        flat_shape = (query_rows, row_count, head_cols)
        query_pre_grad = (
            rotate_back(query_grad, cos_table, sin_table).reshape(flat_shape).astype(jnp.bfloat16)
        )
        key_pre_grad = (
            rotate_back(key_grad, cos_table, sin_table).reshape(flat_shape).astype(jnp.bfloat16)
        )
        value_pre_grad = value_grad.reshape(flat_shape).astype(jnp.bfloat16)
        sum_query_bias = sum_query_bias + jnp.sum(query_pre_grad.astype(jnp.float32), axis=(0, 1))
        sum_key_bias = sum_key_bias + jnp.sum(key_pre_grad.astype(jnp.float32), axis=(0, 1))
        sum_value_bias = sum_value_bias + jnp.sum(value_pre_grad.astype(jnp.float32), axis=(0, 1))
        grad_query = jnp.einsum(
            "srd,src->dc", normed_rows, query_pre_grad, preferred_element_type=jnp.float32
        )
        grad_key = jnp.einsum(
            "srd,src->dc", normed_rows, key_pre_grad, preferred_element_type=jnp.float32
        )
        grad_value = jnp.einsum(
            "srd,src->dc", normed_rows, value_pre_grad, preferred_element_type=jnp.float32
        )
        from_query = jnp.einsum(
            "src,dc->srd", query_pre_grad, full_query, preferred_element_type=jnp.float32
        )
        from_key = jnp.einsum(
            "src,dc->srd", key_pre_grad, full_key, preferred_element_type=jnp.float32
        )
        from_value = jnp.einsum(
            "src,dc->srd", value_pre_grad, full_value, preferred_element_type=jnp.float32
        )
        normed_grad = lax.psum_scatter(
            (from_query + from_key + from_value).astype(jnp.bfloat16),
            "gy",
            scatter_dimension=0,
            tiled=True,
        ).astype(jnp.float32)
        sum_gain_attn = sum_gain_attn + jnp.sum(normed_grad * normal_one, axis=(0, 1))
        sum_shift_attn = sum_shift_attn + jnp.sum(normed_grad, axis=(0, 1))
        input_grad = middle_grad + norm_back(normed_grad, normal_one, factor_one, gain_attn)
        input_grads.append(jnp.transpose(input_grad, (1, 0, 2)))
        reduced = (
            lax.psum_scatter(grad_query, ("dp", "gx"), scatter_dimension=0, tiled=True),
            lax.psum_scatter(grad_key, ("dp", "gx"), scatter_dimension=0, tiled=True),
            lax.psum_scatter(grad_value, ("dp", "gx"), scatter_dimension=0, tiled=True),
            lax.psum_scatter(grad_out, ("dp", "gx"), scatter_dimension=0, tiled=True),
            lax.psum_scatter(grad_up, ("dp", "gx"), scatter_dimension=0, tiled=True),
            lax.psum_scatter(grad_down, ("dp", "gx"), scatter_dimension=0, tiled=True),
        )
        grad_shards = [held + fresh for held, fresh in zip(grad_shards, reduced)]
    query_bias_full = lax.dynamic_update_slice_in_dim(
        jnp.zeros(b_query.shape, jnp.float32), sum_query_bias, head_start, 0
    )
    key_bias_full = lax.dynamic_update_slice_in_dim(
        jnp.zeros(b_key.shape, jnp.float32), sum_key_bias, head_start, 0
    )
    value_bias_full = lax.dynamic_update_slice_in_dim(
        jnp.zeros(b_value.shape, jnp.float32), sum_value_bias, head_start, 0
    )
    up_bias_full = lax.dynamic_update_slice_in_dim(
        jnp.zeros(b_up.shape, jnp.float32), sum_up_bias, up_start, 0
    )
    vectors = lax.psum(
        (
            sum_gain_attn,
            sum_shift_attn,
            query_bias_full,
            key_bias_full,
            value_bias_full,
            sum_out_bias,
            sum_gain_mlp,
            sum_shift_mlp,
            up_bias_full,
            sum_down_bias,
        ),
        ("dp", "gx", "gy"),
    )
    block_output = jnp.stack(outputs)
    input_grad_all = jnp.stack(input_grads)
    return (
        block_output,
        input_grad_all,
        vectors[0],
        vectors[1],
        grad_shards[0],
        vectors[2],
        grad_shards[1],
        vectors[3],
        grad_shards[2],
        vectors[4],
        grad_shards[3],
        vectors[5],
        vectors[6],
        vectors[7],
        grad_shards[4],
        vectors[8],
        grad_shards[5],
        vectors[9],
    )


def solution(mesh):
    placed = (
        P(None, "dp", ("gx", "gy"), None),
        P(None, "dp", None),
        P(None, None, "dp", None),
        P(None, "dp", None),
        P(),
        P(),
        P(("dp", "gx"), "gy"),
        P(),
        P(("dp", "gx"), "gy"),
        P(),
        P(("dp", "gx"), "gy"),
        P(),
        P(("dp", "gx"), "gy"),
        P(),
        P(),
        P(),
        P(("dp", "gx"), "gy"),
        P(),
        P(("dp", "gx"), "gy"),
        P(),
        P(None, "dp", ("gx", "gy"), None),
    )
    return jax.shard_map(
        per_device,
        mesh=mesh,
        in_specs=placed,
        out_specs=(
            P(None, "dp", ("gx", "gy"), None),
            P(None, "dp", ("gx", "gy"), None),
            P(),
            P(),
            P(("dp", "gx"), "gy"),
            P(),
            P(("dp", "gx"), "gy"),
            P(),
            P(("dp", "gx"), "gy"),
            P(),
            P(("dp", "gx"), "gy"),
            P(),
            P(),
            P(),
            P(("dp", "gx"), "gy"),
            P(),
            P(("dp", "gx"), "gy"),
            P(),
        ),
        check_vma=False,
    )
```

profile of v0, /device:TPU:0, one launch (start us, length us, event | category | flops | bytes accessed | tf_op | source)
XLA Modules:
  0.0 1798.1 jit_solution(1486802666801768990)
XLA Ops:
  16.6 36.7 %all_gather.88 = bf16[1280,320]{1,0:T(8,128)(2,1)S(1)} all-gather(bf16[160,320]{1,0:T(8,128)(2,1)S(1)} %copy-done.107), channel_id=1, replica_groups=mesh['dp'=2,'gx'=4,'gy'=4] {'dp','gx'}, dimensions={0}, use_global_device_ids=true | all-gather | bytes 921600 | tf_op jit(solution)/shard_map/all_gather | solution.py:119
  57.5 36.6 %all_gather.85 = bf16[1280,320]{1,0:T(8,128)(2,1)S(1)} all-gather(bf16[160,320]{1,0:T(8,128)(2,1)S(1)} %copy-done.108), channel_id=1, replica_groups=mesh['dp'=2,'gx'=4,'gy'=4] {'dp','gx'}, dimensions={0}, use_global_device_ids=true | all-gather | bytes 921600 | tf_op jit(solution)/shard_map/all_gather | solution.py:120
  108.2 42.6 %all_gather.87 = bf16[1280,320]{1,0:T(8,128)(2,1)} all-gather(bf16[160,320]{1,0:T(8,128)(2,1)} %param.27), channel_id=1, replica_groups=mesh['dp'=2,'gx'=4,'gy'=4] {'dp','gx'}, dimensions={0}, use_global_device_ids=true | all-gather | bytes 921600 | tf_op jit(solution)/shard_map/all_gather | solution.py:118
  154.0 40.2 %all_gather.90 = bf16[1280,320]{1,0:T(8,128)(2,1)} all-gather(bf16[160,320]{1,0:T(8,128)(2,1)} %param.33), channel_id=1, replica_groups=mesh['dp'=2,'gx'=4,'gy'=4] {'dp','gx'}, dimensions={0}, use_global_device_ids=true | all-gather | bytes 921600 | tf_op jit(solution)/shard_map/all_gather | solution.py:121
  283.7 15.2 all-gather.38.cloned.1.call-done
  309.8 25.1 %reduce-scatter.27.cloned.1.call-done = f32[128,1,1280]{2,0,1:T(8,128)} async-done(((f32[512,1,1280]{2,0,1:T(8,128)}), f32[128,1,1280]{2,0,1:T(8,128)}) %reduce-scatter.27.cloned.1.call-update) | async-done | bytes 655376 | tf_op jit(solution)/shard_map/reduce_scatter | solution.py:168
  334.9 37.1 %reduce-scatter.35.cloned.1.call-done = f32[128,1,1280]{2,0,1:T(8,128)} async-done(((f32[512,1,1280]{2,0,1:T(8,128)}), f32[128,1,1280]{2,0,1:T(8,128)}) %reduce-scatter.35.cloned.1.call-update) | async-done | bytes 655376 | tf_op jit(solution)/shard_map/reduce_scatter | solution.py:168
  372.0 36.9 %reduce-scatter.31.cloned.1.call-done = f32[128,1,1280]{2,0,1:T(8,128)} async-done(((f32[512,1,1280]{2,0,1:T(8,128)}), f32[128,1,1280]{2,0,1:T(8,128)}) %reduce-scatter.31.cloned.1.call-update) | async-done | bytes 655376 | tf_op jit(solution)/shard_map/reduce_scatter | solution.py:168
  418.3 12.6 all-gather.30.cloned.1.call-done
  436.6 13.8 all-gather.58.cloned.1.call-done
  450.4 63.4 %all-gather.34.cloned.1.call-done = bf16[1280,1280]{1,0:T(8,128)(2,1)} async-done(((bf16[160,1280]{1,0:T(8,128)(2,1)}), bf16[1280,1280]{1,0:T(8,128)(2,1)}) %all-gather.34.cloned.1.call-update) | async-done | bytes 3276816 | tf_op jit(solution)/shard_map/all_gather | solution.py:123
  538.4 14.0 all-gather.62.cloned.1.call-done
  578.2 13.8 all-gather.60.cloned.1.call-done
  628.8 37.0 %reduce-scatter.55.cloned.1.call-done = f32[128,1,1280]{2,0,1:T(8,128)} async-done(((f32[512,1,1280]{2,0,1:T(8,128)}), f32[128,1,1280]{2,0,1:T(8,128)}) %reduce-scatter.55.cloned.1.call-update) | async-done | bytes 655376 | tf_op jit(solution)/shard_map/reduce_scatter | solution.py:211
  665.7 36.8 %reduce-scatter.47.cloned.1.call-done = f32[128,1,1280]{2,0,1:T(8,128)} async-done(((f32[512,1,1280]{2,0,1:T(8,128)}), f32[128,1,1280]{2,0,1:T(8,128)}) %reduce-scatter.47.cloned.1.call-update) | async-done | bytes 655376 | tf_op jit(solution)/shard_map/reduce_scatter | solution.py:211
  705.4 26.1 %reduce-scatter.33.cloned.1.call-done = bf16[128,1,1280]{2,0,1:T(8,128)(2,1)} async-done(((bf16[512,1,1280]{2,0,1:T(8,128)(2,1)}), bf16[128,1,1280]{2,0,1:T(8,128)(2,1)}) %reduce-scatter.33.cloned.1.call-update) | async-done | bytes 327696 | tf_op jit(solution)/shard_map/reduce_scatter | solution.py:186
  735.2 25.7 %reduce-scatter.37.cloned.1.call-done = bf16[128,1,1280]{2,0,1:T(8,128)(2,1)} async-done(((bf16[512,1,1280]{2,0,1:T(8,128)(2,1)}), bf16[128,1,1280]{2,0,1:T(8,128)(2,1)}) %reduce-scatter.37.cloned.1.call-update) | async-done | bytes 327696 | tf_op jit(solution)/shard_map/reduce_scatter | solution.py:186
  760.8 28.9 %reduce-scatter.29.cloned.1.call-done = bf16[128,1,1280]{2,0,1:T(8,128)(2,1)} async-done(((bf16[512,1,1280]{2,0,1:T(8,128)(2,1)}), bf16[128,1,1280]{2,0,1:T(8,128)(2,1)}) %reduce-scatter.29.cloned.1.call-update) | async-done | bytes 327696 | tf_op jit(solution)/shard_map/reduce_scatter | solution.py:186
  797.4 14.0 multiply_reduce_fusion.1
  843.3 13.8 multiply_reduce_fusion.2
  888.8 13.8 multiply_reduce_fusion
  963.2 31.7 %reduce-scatter.41.cloned.1.call-done = f32[512,1,4,80]{0,3,2,1:T(8,128)} async-done(((f32[2048,1,4,80]{0,3,2,1:T(8,128)}), f32[512,1,4,80]{0,3,2,1:T(8,128)}) %reduce-scatter.41.cloned.1.call-update) | async-done | bytes 655376 | tf_op jit(solution)/shard_map/reduce_scatter | solution.py:252
  997.0 52.1 %reduce-scatter.43.cloned.1.call-done = f32[512,1,4,80]{0,3,2,1:T(8,128)} async-done(((f32[2048,1,4,80]{0,3,2,1:T(8,128)}), f32[512,1,4,80]{0,3,2,1:T(8,128)}) %reduce-scatter.43.cloned.1.call-update) | async-done | bytes 655376 | tf_op jit(solution)/shard_map/reduce_scatter | solution.py:253
  1065.4 37.7 %reduce-scatter.57.cloned.1.call-done = f32[512,1,4,80]{0,3,2,1:T(8,128)} async-done(((f32[2048,1,4,80]{0,3,2,1:T(8,128)}), f32[512,1,4,80]{0,3,2,1:T(8,128)}) %reduce-scatter.57.cloned.1.call-update) | async-done | bytes 655376 | tf_op jit(solution)/shard_map/reduce_scatter | solution.py:252
  1105.1 52.1 %reduce-scatter.59.cloned.1.call-done = f32[512,1,4,80]{0,3,2,1:T(8,128)} async-done(((f32[2048,1,4,80]{0,3,2,1:T(8,128)}), f32[512,1,4,80]{0,3,2,1:T(8,128)}) %reduce-scatter.59.cloned.1.call-update) | async-done | bytes 655376 | tf_op jit(solution)/shard_map/reduce_scatter | solution.py:253
  1215.1 28.4 %reduce-scatter.61.cloned.1.call-done = bf16[128,1,1280]{2,0,1:T(8,128)(2,1)} async-done(((bf16[512,1,1280]{2,0,1:T(8,128)(2,1)}), bf16[128,1,1280]{2,0,1:T(8,128)(2,1)}) %reduce-scatter.61.cloned.1.call-update) | async-done | bytes 327696 | tf_op jit(solution)/shard_map/reduce_scatter | solution.py:284
  1262.2 53.0 %reduce-scatter.69.cloned.1.call-done = f32[160,320]{1,0:T(8,128)} async-done(((f32[1280,320]{1,0:T(8,128)}), f32[160,320]{1,0:T(8,128)}) %reduce-scatter.69.cloned.1.call-update) | async-done | bytes 204816 | tf_op jit(solution)/shard_map/reduce_scatter | solution.py:298
  1315.2 70.8 %reduce-scatter.63.cloned.1.call-done = f32[160,320]{1,0:T(8,128)} async-done(((f32[1280,320]{1,0:T(8,128)}), f32[160,320]{1,0:T(8,128)}) %reduce-scatter.63.cloned.1.call-update) | async-done | bytes 204816 | tf_op jit(solution)/shard_map/reduce_scatter | solution.py:295
  1386.0 124.7 %reduce-scatter.73.cloned.1.call-done = f32[160,1280]{1,0:T(8,128)} async-done(((f32[1280,1280]{1,0:T(8,128)}), f32[160,1280]{1,0:T(8,128)}) %reduce-scatter.73.cloned.1.call-update) | async-done | bytes 819216
  1510.7 125.2 %reduce-scatter.71.cloned.1.call-done = f32[160,1280]{1,0:T(8,128)} async-done(((f32[1280,1280]{1,0:T(8,128)}), f32[160,1280]{1,0:T(8,128)}) %reduce-scatter.71.cloned.1.call-update) | async-done | bytes 819216 | tf_op jit(solution)/shard_map/reduce_scatter | solution.py:299
  1635.9 70.9 %reduce-scatter.67.cloned.1.call-done = f32[160,320]{1,0:T(8,128)} async-done(((f32[1280,320]{1,0:T(8,128)}), f32[160,320]{1,0:T(8,128)}) %reduce-scatter.67.cloned.1.call-update) | async-done | bytes 204816 | tf_op jit(solution)/shard_map/reduce_scatter | solution.py:297
  1706.8 70.3 %reduce-scatter.65.cloned.1.call-done = f32[160,320]{1,0:T(8,128)} async-done(((f32[1280,320]{1,0:T(8,128)}), f32[160,320]{1,0:T(8,128)}) %reduce-scatter.65.cloned.1.call-update) | async-done | bytes 204816 | tf_op jit(solution)/shard_map/reduce_scatter | solution.py:296
  (685 shorter events, 477.9 us)
Async XLA Ops:
  14.8 189.1 %all-gather.28.cloned.1.call-start = ((), (), s32[]{:S(2)}) async-start(), calls=%async_computation.26 | async-start | bytes 1638400 | tf_op jit(solution)/shard_map/all_gather | solution.py:146
  56.7 164.6 %all-gather.26.cloned.1.call-start = ((), (), s32[]{:S(2)}) async-start(), calls=%async_computation.25 | async-start | bytes 1638400 | tf_op jit(solution)/shard_map/all_gather | solution.py:147
  97.2 137.1 %all-gather.48.cloned.1.call-start = ((), (), s32[]{:S(2)}) async-start(), calls=%async_computation.40 | async-start | bytes 1638400 | tf_op jit(solution)/shard_map/all_gather | solution.py:146
  101.0 151.1 %all-gather.46.cloned.1.call-start = ((), (), s32[]{:S(2)}) async-start(), calls=%async_computation.39 | async-start | bytes 1638400 | tf_op jit(solution)/shard_map/all_gather | solution.py:147
  105.7 160.3 %all-gather.40.cloned.1.call-start = ((), (), s32[]{:S(2)}) async-start(), calls=%async_computation.34 | async-start | bytes 1638400 | tf_op jit(solution)/shard_map/all_gather | solution.py:146
  154.0 144.9 %all-gather.38.cloned.1.call-start = ((), (), s32[]{:S(2)}) async-start(), calls=%async_computation.33 | async-start | bytes 1638400 | tf_op jit(solution)/shard_map/all_gather | solution.py:147
  231.7 140.3 %reduce-scatter.35.cloned.1.call-start = ((), (), s32[]{:S(2)}) async-start(), calls=%async_computation.41 | async-start | bytes 3276800 | tf_op jit(solution)/shard_map/reduce_scatter | solution.py:168
  263.3 145.7 %reduce-scatter.31.cloned.1.call-start = ((), (), s32[]{:S(2)}) async-start(), calls=%async_computation.35 | async-start | bytes 3276800 | tf_op jit(solution)/shard_map/reduce_scatter | solution.py:168
  415.3 137.0 %all-gather.62.cloned.1.call-start = ((), (), s32[]{:S(2)}) async-start(), calls=%async_computation.61 | async-start | bytes 1638400 | tf_op jit(solution)/shard_map/all_gather | solution.py:199
  416.1 156.4 %all-gather.42.cloned.1.call-start = ((), (), s32[]{:S(2)}) async-start(), calls=%async_computation.36 | async-start | bytes 1638400 | tf_op jit(solution)/shard_map/all_gather | solution.py:178
  416.7 175.3 %all-gather.60.cloned.1.call-start = ((), (), s32[]{:S(2)}) async-start(), calls=%async_computation.60 | async-start | bytes 1638400 | tf_op jit(solution)/shard_map/all_gather | solution.py:199
  417.2 211.5 %reduce-scatter.39.cloned.1.call-start = ((), (), s32[]{:S(2)}) async-start(), calls=%async_computation.44 | async-start | bytes 3276800 | tf_op jit(solution)/shard_map/reduce_scatter | solution.py:211
  524.5 141.2 %reduce-scatter.55.cloned.1.call-start = ((), (), s32[]{:S(2)}) async-start(), calls=%async_computation.54 | async-start | bytes 3276800 | tf_op jit(solution)/shard_map/reduce_scatter | solution.py:211
  563.1 139.4 %reduce-scatter.47.cloned.1.call-start = ((), (), s32[]{:S(2)}) async-start(), calls=%async_computation.49 | async-start | bytes 3276800 | tf_op jit(solution)/shard_map/reduce_scatter | solution.py:211
  609.0 151.9 %reduce-scatter.37.cloned.1.call-start = ((), (), s32[]{:S(2)}) async-start(), calls=%async_computation.43 | async-start | bytes 1638400 | tf_op jit(solution)/shard_map/reduce_scatter | solution.py:186
  615.2 174.6 %reduce-scatter.29.cloned.1.call-start = ((), (), s32[]{:S(2)}) async-start(), calls=%async_computation.31 | async-start | bytes 1638400 | tf_op jit(solution)/shard_map/reduce_scatter | solution.py:186
  621.3 173.4 %all-gather.54.cloned.1.call-start = ((), (), s32[]{:S(2)}) async-start(), calls=%async_computation.50 | async-start | bytes 1638400 | tf_op jit(solution)/shard_map/all_gather | solution.py:224
  794.6 150.2 %reduce-scatter.49.cloned.1.call-start = ((), (), s32[]{:S(2)}) async-start(), calls=%async_computation.51 | async-start | bytes 3276800 | tf_op jit(solution)/shard_map/reduce_scatter | solution.py:252
  839.8 155.2 %reduce-scatter.41.cloned.1.call-start = ((), (), s32[]{:S(2)}) async-start(), calls=%async_computation.46 | async-start | bytes 3276800 | tf_op jit(solution)/shard_map/reduce_scatter | solution.py:252
  874.3 174.8 %reduce-scatter.43.cloned.1.call-start = ((), (), s32[]{:S(2)}) async-start(), calls=%async_computation.47 | async-start | bytes 3276800 | tf_op jit(solution)/shard_map/reduce_scatter | solution.py:253
  885.4 217.7 %reduce-scatter.57.cloned.1.call-start = ((), (), s32[]{:S(2)}) async-start(), calls=%async_computation.56 | async-start | bytes 3276800 | tf_op jit(solution)/shard_map/reduce_scatter | solution.py:252
  920.0 237.2 %reduce-scatter.59.cloned.1.call-start = ((), (), s32[]{:S(2)}) async-start(), calls=%async_computation.57 | async-start | bytes 3276800 | tf_op jit(solution)/shard_map/reduce_scatter | solution.py:253
  931.1 284.0 %reduce-scatter.53.cloned.1.call-start = ((), (), s32[]{:S(2)}) async-start(), calls=%async_computation.53 | async-start | bytes 1638400 | tf_op jit(solution)/shard_map/reduce_scatter | solution.py:284
  952.9 262.2 %reduce-scatter.45.cloned.1.call-start = ((), (), s32[]{:S(2)}) async-start(), calls=%async_computation.48 | async-start | bytes 1638400 | tf_op jit(solution)/shard_map/reduce_scatter | solution.py:284
  1055.0 188.6 %reduce-scatter.61.cloned.1.call-start = ((), (), s32[]{:S(2)}) async-start(), calls=%async_computation.58 | async-start | bytes 1638400 | tf_op jit(solution)/shard_map/reduce_scatter | solution.py:284
  1163.2 152.0 %reduce-scatter.69.cloned.1.call-start = ((), (), s32[]{:S(2)}) async-start(), calls=%async_computation.65 | async-start | bytes 2211840 | tf_op jit(solution)/shard_map/reduce_scatter | solution.py:298
  1169.6 216.4 %reduce-scatter.63.cloned.1.call-start = ((), (), s32[]{:S(2)}) async-start(), calls=%async_computation.62 | async-start | bytes 2211840 | tf_op jit(solution)/shard_map/reduce_scatter | solution.py:295
  1175.1 335.5 %reduce-scatter.73.cloned.1.call-start = ((), (), s32[]{:S(2)}) async-start(), calls=%async_computation.67 | async-start | bytes 7372800
  1194.6 441.3 %reduce-scatter.71.cloned.1.call-start = ((), (), s32[]{:S(2)}) async-start(), calls=%async_computation.66 | async-start | bytes 7372800 | tf_op jit(solution)/shard_map/reduce_scatter | solution.py:299
  1205.6 430.2 %all-reduce.3.cloned.1.call-start = ((), (), s32[]{:S(2)}) async-start(), calls=%async_computation.68 | async-start | bytes 188416 | tf_op jit(solution)/shard_map/psum | solution.py:315
  1247.0 459.8 %reduce-scatter.67.cloned.1.call-start = ((), (), s32[]{:S(2)}) async-start(), calls=%async_computation.64 | async-start | bytes 2211840 | tf_op jit(solution)/shard_map/reduce_scatter | solution.py:297
  1251.2 525.9 %reduce-scatter.65.cloned.1.call-start = ((), (), s32[]{:S(2)}) async-start(), calls=%async_computation.63 | async-start | bytes 2211840 | tf_op jit(solution)/shard_map/reduce_scatter | solution.py:296
  (197 other events, 4502.2 us)
Sparse Core Ops, SparseCore 0:
  13.4 20.8 all-gather.23
  36.5 18.1 all-gather.43
  56.8 18.1 all-gather.35
  76.4 38.0 all-gather.27
  115.9 43.1 all-gather.25
  160.6 37.9 all-gather.47
  200.2 32.1 all-gather.45
  233.9 31.7 all-gather.39
  267.3 31.5 all-gather.37
  301.3 33.6 reduce-scatter.26
  337.5 34.4 reduce-scatter.34
  374.4 34.4 reduce-scatter.30
  734.8 18.1 all-gather.53
  794.1 18.1 all-gather.51
  814.3 18.1 all-gather.55
  834.7 52.2 reduce-scatter.48
  889.1 51.7 reduce-scatter.50
  943.1 51.7 reduce-scatter.40
  997.2 51.7 reduce-scatter.42
  1051.2 51.7 reduce-scatter.56
  1105.4 51.7 reduce-scatter.58
  1159.7 25.9 reduce-scatter.52
  1188.3 26.4 reduce-scatter.44
  1217.1 26.3 reduce-scatter.60
  1247.6 67.5 reduce-scatter.68
  1319.1 66.8 reduce-scatter.62
  1390.0 120.6 reduce-scatter.72
  1514.9 120.9 reduce-scatter.70
  1639.9 66.8 reduce-scatter.66
  1710.7 66.3 reduce-scatter.64
Sparse Core Ops, SparseCore 1:
  311.8 60.4 all-gather.31
  412.8 18.0 all-gather.29
  432.3 18.0 all-gather.57
  452.5 61.3 all-gather.33
  516.0 16.7 all-gather.49
  534.3 18.0 all-gather.61
  554.4 18.0 all-gather.41
  573.9 18.0 all-gather.59
  594.3 34.4 reduce-scatter.38
  631.3 34.4 reduce-scatter.54
  668.1 34.3 reduce-scatter.46
  705.1 26.3 reduce-scatter.32
  734.4 26.3 reduce-scatter.36
  763.4 26.3 reduce-scatter.28
  1247.1 138.3 all-reduce.2
where the time goes:
time: 1810 us; the launch traced here: 1800 us
  waiting for transfers between devices  1130 us (62%)
  matrix products  311 us (17%)
  blocking collectives  156 us (9%)
  other arithmetic  111 us (6%)
  local copies, waits for them, and re-layouts  61.2 us (3%)
  between operations  19.2 us (1%)
    unnamed x46, waiting for transfers between devices  131 us
    reduce_scatter x1, waiting for transfers between devices, per_device(): lax.psum_scatter(grad_up, ('dp', 'gx'), scatter_dimension=0, tiled=True)  125 us
    reduce_scatter x3, waiting for transfers between devices, per_device(): lax.psum_scatter(value_part, 'gx', scatter_dimension=0, tiled=True)  104 us
    reduce_scatter x3, waiting for transfers between devices, per_device(): lax.psum_scatter(jnp.einsum('srh,oh->sro', mixture, full_out, preferred_e...  99.1 us
    reduce_scatter x3, waiting for transfers between devices, per_device(): lax.psum_scatter(jnp.einsum('srf,df->srd', hidden_grad, full_up, preferre...  81.2 us
    reduce_scatter x3, waiting for transfers between devices, per_device(): lax.psum_scatter(jnp.einsum('srf,of->sro', active, full_down, preferred_e...  80.7 us
    reduce_scatter x1, waiting for transfers between devices, per_device(): lax.psum_scatter(grad_value, ('dp', 'gx'), scatter_dimension=0, tiled=True)  70.9 us
    reduce_scatter x1, waiting for transfers between devices, per_device(): lax.psum_scatter(grad_query, ('dp', 'gx'), scatter_dimension=0, tiled=True)  70.8 us
  transfers between devices with their start and end apart: 45, of which 28 were waited for; matrix products, arithmetic and copies ran while one was open for 24% of the time, Pallas kernels for 0%

commit v1 on v0

--- a/solution.py
+++ b/solution.py
@@ -5,6 +5,23 @@
 
 HEAD_DIM = 80
 EPSILON = 1e-06
+
+
+def define_quarters(body, shard_axis):
+    q_next, k_now, finding = (
+        lax.psum(1, axis_name=shard_axis),
+        lax.axis_index(shard_axis),
+        body.shape[0],
+    )
+    small = jnp.zeros((*body.shape[:0], q_next * finding, *body.shape[1:]), body.dtype)
+    runs = tuple(((q, (q + 1) % q_next) for q in range(q_next)))
+    v_now = body
+    for to_i in range(q_next):
+        v_next = (k_now - to_i) % q_next
+        small = lax.dynamic_update_slice_in_dim(small, v_now, v_next * finding, axis=0)
+        if to_i < q_next - 1:
+            v_now = lax.ppermute(v_now, axis_name=shard_axis, perm=runs)
+    return small
 
 
 def layer_norm(values, norm_gain, norm_shift):
@@ -117,7 +134,7 @@
         blocks = (
             lax.all_gather(w_query, ("dp", "gx"), axis=0, tiled=True),
             lax.all_gather(w_key, ("dp", "gx"), axis=0, tiled=True),
-            lax.all_gather(w_value, ("dp", "gx"), axis=0, tiled=True),
+            define_quarters(w_value, ("dp", "gx")),
             lax.all_gather(w_out, ("dp", "gx"), axis=0, tiled=True),
             lax.all_gather(w_up, ("dp", "gx"), axis=0, tiled=True),
             lax.all_gather(w_down, ("dp", "gx"), axis=0, tiled=True),

time: 1810 us -> 1820 us (level)
  waiting for transfers between devices: 1130 us -> 1180 us
  blocking collectives: 156 us -> 120 us
    ppermute x0 -> x7, waiting for transfers between devices: none -> 57.3 us  [define_quarters(): v_now = lax.ppermute(v_now, axis_name=shard_axis, perm=runs)]
    all_gather x1 -> x0, blocking collectives: 36.6 us -> none  [per_device(): lax.all_gather(w_value, ('dp', 'gx'), axis=0, tiled=True)]
    unnamed x379 -> x383, local copies, waits for them, and re-layouts: 54.4 us -> 55.6 us
  transfers between devices with their start and end apart: 45 -> 52, of which waited for: 28 -> 35; matrix products, arithmetic and copies ran while one was open for 24% -> 24% of each run, Pallas kernels for 0% -> 0%
where the time goes in v1:
time: 1820 us; the launch traced here: 1810 us
  waiting for transfers between devices  1180 us (65%)
  matrix products  311 us (17%)
  blocking collectives  120 us (7%)
  other arithmetic  112 us (6%)
  local copies, waits for them, and re-layouts  62.7 us (3%)
  between operations  18.9 us (1%)
    unnamed x46, waiting for transfers between devices  131 us
    reduce_scatter x1, waiting for transfers between devices, per_device(): lax.psum_scatter(grad_up, ('dp', 'gx'), scatter_dimension=0, tiled=True)  125 us
    reduce_scatter x3, waiting for transfers between devices, per_device(): lax.psum_scatter(value_part, 'gx', scatter_dimension=0, tiled=True)  104 us
    reduce_scatter x3, waiting for transfers between devices, per_device(): lax.psum_scatter(jnp.einsum('srh,oh->sro', mixture, full_out, preferred_e...  99 us
    reduce_scatter x3, waiting for transfers between devices, per_device(): lax.psum_scatter(jnp.einsum('srf,df->srd', hidden_grad, full_up, preferre...  81.2 us
    reduce_scatter x3, waiting for transfers between devices, per_device(): lax.psum_scatter(jnp.einsum('srf,of->sro', active, full_down, preferred_e...  80.8 us
    reduce_scatter x1, waiting for transfers between devices, per_device(): lax.psum_scatter(grad_value, ('dp', 'gx'), scatter_dimension=0, tiled=True)  70.9 us
    reduce_scatter x1, waiting for transfers between devices, per_device(): lax.psum_scatter(grad_query, ('dp', 'gx'), scatter_dimension=0, tiled=True)  70.8 us
  transfers between devices with their start and end apart: 52, of which 35 were waited for; matrix products, arithmetic and copies ran while one was open for 24% of the time, Pallas kernels for 0%

profile of v1, /device:TPU:0, one launch (start us, length us, event | category | flops | bytes accessed | tf_op | source)
XLA Modules:
  0.0 1808.9 jit_solution(3221076875394601054)
XLA Ops:
  17.8 36.7 %all_gather.82 = bf16[1280,320]{1,0:T(8,128)(2,1)S(1)} all-gather(bf16[160,320]{1,0:T(8,128)(2,1)S(1)} %copy-done.108), channel_id=1, replica_groups=mesh['dp'=2,'gx'=4,'gy'=4] {'dp','gx'}, dimensions={0}, use_global_device_ids=true | all-gather | bytes 921600 | tf_op jit(solution)/shard_map/all_gather | solution.py:136
  89.2 10.4 collective-permute-done.4
  99.6 10.3 collective-permute-done.5
  131.6 41.9 %all_gather.81 = bf16[1280,320]{1,0:T(8,128)(2,1)} all-gather(bf16[160,320]{1,0:T(8,128)(2,1)} %param.27), channel_id=1, replica_groups=mesh['dp'=2,'gx'=4,'gy'=4] {'dp','gx'}, dimensions={0}, use_global_device_ids=true | all-gather | bytes 921600 | tf_op jit(solution)/shard_map/all_gather | solution.py:135
  176.7 41.5 %all_gather.84 = bf16[1280,320]{1,0:T(8,128)(2,1)} all-gather(bf16[160,320]{1,0:T(8,128)(2,1)} %param.33), channel_id=1, replica_groups=mesh['dp'=2,'gx'=4,'gy'=4] {'dp','gx'}, dimensions={0}, use_global_device_ids=true | all-gather | bytes 921600 | tf_op jit(solution)/shard_map/all_gather | solution.py:138
  320.8 25.1 %reduce-scatter.27.cloned.1.call-done = f32[128,1,1280]{2,0,1:T(8,128)} async-done(((f32[512,1,1280]{2,0,1:T(8,128)}), f32[128,1,1280]{2,0,1:T(8,128)}) %reduce-scatter.27.cloned.1.call-update) | async-done | bytes 655376 | tf_op jit(solution)/shard_map/reduce_scatter | solution.py:185
  345.9 37.1 %reduce-scatter.35.cloned.1.call-done = f32[128,1,1280]{2,0,1:T(8,128)} async-done(((f32[512,1,1280]{2,0,1:T(8,128)}), f32[128,1,1280]{2,0,1:T(8,128)}) %reduce-scatter.35.cloned.1.call-update) | async-done | bytes 655376 | tf_op jit(solution)/shard_map/reduce_scatter | solution.py:185
  382.9 36.9 %reduce-scatter.31.cloned.1.call-done = f32[128,1,1280]{2,0,1:T(8,128)} async-done(((f32[512,1,1280]{2,0,1:T(8,128)}), f32[128,1,1280]{2,0,1:T(8,128)}) %reduce-scatter.31.cloned.1.call-update) | async-done | bytes 655376 | tf_op jit(solution)/shard_map/reduce_scatter | solution.py:185
  429.2 12.6 all-gather.30.cloned.1.call-done
  447.5 13.8 all-gather.58.cloned.1.call-done
  461.3 63.4 %all-gather.34.cloned.1.call-done = bf16[1280,1280]{1,0:T(8,128)(2,1)} async-done(((bf16[160,1280]{1,0:T(8,128)(2,1)}), bf16[1280,1280]{1,0:T(8,128)(2,1)}) %all-gather.34.cloned.1.call-update) | async-done | bytes 3276816 | tf_op jit(solution)/shard_map/all_gather | solution.py:140
  549.3 14.0 all-gather.62.cloned.1.call-done
  589.1 13.8 all-gather.60.cloned.1.call-done
  639.6 37.0 %reduce-scatter.55.cloned.1.call-done = f32[128,1,1280]{2,0,1:T(8,128)} async-done(((f32[512,1,1280]{2,0,1:T(8,128)}), f32[128,1,1280]{2,0,1:T(8,128)}) %reduce-scatter.55.cloned.1.call-update) | async-done | bytes 655376 | tf_op jit(solution)/shard_map/reduce_scatter | solution.py:228
  676.6 36.8 %reduce-scatter.47.cloned.1.call-done = f32[128,1,1280]{2,0,1:T(8,128)} async-done(((f32[512,1,1280]{2,0,1:T(8,128)}), f32[128,1,1280]{2,0,1:T(8,128)}) %reduce-scatter.47.cloned.1.call-update) | async-done | bytes 655376 | tf_op jit(solution)/shard_map/reduce_scatter | solution.py:228
  716.4 26.1 %reduce-scatter.33.cloned.1.call-done = bf16[128,1,1280]{2,0,1:T(8,128)(2,1)} async-done(((bf16[512,1,1280]{2,0,1:T(8,128)(2,1)}), bf16[128,1,1280]{2,0,1:T(8,128)(2,1)}) %reduce-scatter.33.cloned.1.call-update) | async-done | bytes 327696 | tf_op jit(solution)/shard_map/reduce_scatter | solution.py:203
  745.9 25.9 %reduce-scatter.37.cloned.1.call-done = bf16[128,1,1280]{2,0,1:T(8,128)(2,1)} async-done(((bf16[512,1,1280]{2,0,1:T(8,128)(2,1)}), bf16[128,1,1280]{2,0,1:T(8,128)(2,1)}) %reduce-scatter.37.cloned.1.call-update) | async-done | bytes 327696 | tf_op jit(solution)/shard_map/reduce_scatter | solution.py:203
  771.8 28.9 %reduce-scatter.29.cloned.1.call-done = bf16[128,1,1280]{2,0,1:T(8,128)(2,1)} async-done(((bf16[512,1,1280]{2,0,1:T(8,128)(2,1)}), bf16[128,1,1280]{2,0,1:T(8,128)(2,1)}) %reduce-scatter.29.cloned.1.call-update) | async-done | bytes 327696 | tf_op jit(solution)/shard_map/reduce_scatter | solution.py:203
  808.3 14.0 multiply_reduce_fusion.1
  854.3 13.8 multiply_reduce_fusion.2
  899.8 13.8 multiply_reduce_fusion
  974.0 31.9 %reduce-scatter.41.cloned.1.call-done = f32[512,1,4,80]{0,3,2,1:T(8,128)} async-done(((f32[2048,1,4,80]{0,3,2,1:T(8,128)}), f32[512,1,4,80]{0,3,2,1:T(8,128)}) %reduce-scatter.41.cloned.1.call-update) | async-done | bytes 655376 | tf_op jit(solution)/shard_map/reduce_scatter | solution.py:269
  1007.9 52.1 %reduce-scatter.43.cloned.1.call-done = f32[512,1,4,80]{0,3,2,1:T(8,128)} async-done(((f32[2048,1,4,80]{0,3,2,1:T(8,128)}), f32[512,1,4,80]{0,3,2,1:T(8,128)}) %reduce-scatter.43.cloned.1.call-update) | async-done | bytes 655376 | tf_op jit(solution)/shard_map/reduce_scatter | solution.py:270
  1076.3 37.7 %reduce-scatter.57.cloned.1.call-done = f32[512,1,4,80]{0,3,2,1:T(8,128)} async-done(((f32[2048,1,4,80]{0,3,2,1:T(8,128)}), f32[512,1,4,80]{0,3,2,1:T(8,128)}) %reduce-scatter.57.cloned.1.call-update) | async-done | bytes 655376 | tf_op jit(solution)/shard_map/reduce_scatter | solution.py:269
  1116.0 52.1 %reduce-scatter.59.cloned.1.call-done = f32[512,1,4,80]{0,3,2,1:T(8,128)} async-done(((f32[2048,1,4,80]{0,3,2,1:T(8,128)}), f32[512,1,4,80]{0,3,2,1:T(8,128)}) %reduce-scatter.59.cloned.1.call-update) | async-done | bytes 655376 | tf_op jit(solution)/shard_map/reduce_scatter | solution.py:270
  1226.3 28.1 %reduce-scatter.61.cloned.1.call-done = bf16[128,1,1280]{2,0,1:T(8,128)(2,1)} async-done(((bf16[512,1,1280]{2,0,1:T(8,128)(2,1)}), bf16[128,1,1280]{2,0,1:T(8,128)(2,1)}) %reduce-scatter.61.cloned.1.call-update) | async-done | bytes 327696 | tf_op jit(solution)/shard_map/reduce_scatter | solution.py:301
  1272.9 53.2 %reduce-scatter.69.cloned.1.call-done = f32[160,320]{1,0:T(8,128)} async-done(((f32[1280,320]{1,0:T(8,128)}), f32[160,320]{1,0:T(8,128)}) %reduce-scatter.69.cloned.1.call-update) | async-done | bytes 204816 | tf_op jit(solution)/shard_map/reduce_scatter | solution.py:315
  1326.0 70.8 %reduce-scatter.63.cloned.1.call-done = f32[160,320]{1,0:T(8,128)} async-done(((f32[1280,320]{1,0:T(8,128)}), f32[160,320]{1,0:T(8,128)}) %reduce-scatter.63.cloned.1.call-update) | async-done | bytes 204816 | tf_op jit(solution)/shard_map/reduce_scatter | solution.py:312
  1396.9 124.7 %reduce-scatter.73.cloned.1.call-done = f32[160,1280]{1,0:T(8,128)} async-done(((f32[1280,1280]{1,0:T(8,128)}), f32[160,1280]{1,0:T(8,128)}) %reduce-scatter.73.cloned.1.call-update) | async-done | bytes 819216
  1521.6 125.2 %reduce-scatter.71.cloned.1.call-done = f32[160,1280]{1,0:T(8,128)} async-done(((f32[1280,1280]{1,0:T(8,128)}), f32[160,1280]{1,0:T(8,128)}) %reduce-scatter.71.cloned.1.call-update) | async-done | bytes 819216 | tf_op jit(solution)/shard_map/reduce_scatter | solution.py:316
  1646.8 70.9 %reduce-scatter.67.cloned.1.call-done = f32[160,320]{1,0:T(8,128)} async-done(((f32[1280,320]{1,0:T(8,128)}), f32[160,320]{1,0:T(8,128)}) %reduce-scatter.67.cloned.1.call-update) | async-done | bytes 204816 | tf_op jit(solution)/shard_map/reduce_scatter | solution.py:314
  1717.7 70.4 %reduce-scatter.65.cloned.1.call-done = f32[160,320]{1,0:T(8,128)} async-done(((f32[1280,320]{1,0:T(8,128)}), f32[160,320]{1,0:T(8,128)}) %reduce-scatter.65.cloned.1.call-update) | async-done | bytes 204816 | tf_op jit(solution)/shard_map/reduce_scatter | solution.py:313
  (711 shorter events, 519.2 us)
Async XLA Ops:
  14.1 159.5 %all-gather.36.cloned.1.call-start = ((), (), s32[]{:S(2)}) async-start(), calls=%async_computation.32 | async-start | bytes 1638400 | tf_op jit(solution)/shard_map/all_gather | solution.py:145
  14.8 212.9 %all-gather.28.cloned.1.call-start = ((), (), s32[]{:S(2)}) async-start(), calls=%async_computation.26 | async-start | bytes 1638400 | tf_op jit(solution)/shard_map/all_gather | solution.py:163
  57.8 187.1 %all-gather.26.cloned.1.call-start = ((), (), s32[]{:S(2)}) async-start(), calls=%async_computation.25 | async-start | bytes 1638400 | tf_op jit(solution)/shard_map/all_gather | solution.py:164
  120.6 138.5 %all-gather.48.cloned.1.call-start = ((), (), s32[]{:S(2)}) async-start(), calls=%async_computation.40 | async-start | bytes 1638400 | tf_op jit(solution)/shard_map/all_gather | solution.py:163
  124.3 152.3 %all-gather.46.cloned.1.call-start = ((), (), s32[]{:S(2)}) async-start(), calls=%async_computation.39 | async-start | bytes 1638400 | tf_op jit(solution)/shard_map/all_gather | solution.py:164
  129.1 161.2 %all-gather.40.cloned.1.call-start = ((), (), s32[]{:S(2)}) async-start(), calls=%async_computation.34 | async-start | bytes 1638400 | tf_op jit(solution)/shard_map/all_gather | solution.py:163
  176.7 133.2 %all-gather.38.cloned.1.call-start = ((), (), s32[]{:S(2)}) async-start(), calls=%async_computation.33 | async-start | bytes 1638400 | tf_op jit(solution)/shard_map/all_gather | solution.py:164
  287.8 132.1 %reduce-scatter.31.cloned.1.call-start = ((), (), s32[]{:S(2)}) async-start(), calls=%async_computation.35 | async-start | bytes 3276800 | tf_op jit(solution)/shard_map/reduce_scatter | solution.py:185
  426.3 137.0 %all-gather.62.cloned.1.call-start = ((), (), s32[]{:S(2)}) async-start(), calls=%async_computation.61 | async-start | bytes 1638400 | tf_op jit(solution)/shard_map/all_gather | solution.py:216
  427.0 156.4 %all-gather.42.cloned.1.call-start = ((), (), s32[]{:S(2)}) async-start(), calls=%async_computation.36 | async-start | bytes 1638400 | tf_op jit(solution)/shard_map/all_gather | solution.py:195
  427.6 175.3 %all-gather.60.cloned.1.call-start = ((), (), s32[]{:S(2)}) async-start(), calls=%async_computation.60 | async-start | bytes 1638400 | tf_op jit(solution)/shard_map/all_gather | solution.py:216
  428.2 211.4 %reduce-scatter.39.cloned.1.call-start = ((), (), s32[]{:S(2)}) async-start(), calls=%async_computation.44 | async-start | bytes 3276800 | tf_op jit(solution)/shard_map/reduce_scatter | solution.py:228
  535.4 141.2 %reduce-scatter.55.cloned.1.call-start = ((), (), s32[]{:S(2)}) async-start(), calls=%async_computation.54 | async-start | bytes 3276800 | tf_op jit(solution)/shard_map/reduce_scatter | solution.py:228
  574.1 139.4 %reduce-scatter.47.cloned.1.call-start = ((), (), s32[]{:S(2)}) async-start(), calls=%async_computation.49 | async-start | bytes 3276800 | tf_op jit(solution)/shard_map/reduce_scatter | solution.py:228
  619.9 151.9 %reduce-scatter.37.cloned.1.call-start = ((), (), s32[]{:S(2)}) async-start(), calls=%async_computation.43 | async-start | bytes 1638400 | tf_op jit(solution)/shard_map/reduce_scatter | solution.py:203
  626.1 174.6 %reduce-scatter.29.cloned.1.call-start = ((), (), s32[]{:S(2)}) async-start(), calls=%async_computation.31 | async-start | bytes 1638400 | tf_op jit(solution)/shard_map/reduce_scatter | solution.py:203
  632.2 173.4 %all-gather.54.cloned.1.call-start = ((), (), s32[]{:S(2)}) async-start(), calls=%async_computation.50 | async-start | bytes 1638400 | tf_op jit(solution)/shard_map/all_gather | solution.py:241
  805.5 150.3 %reduce-scatter.49.cloned.1.call-start = ((), (), s32[]{:S(2)}) async-start(), calls=%async_computation.51 | async-start | bytes 3276800 | tf_op jit(solution)/shard_map/reduce_scatter | solution.py:269
  850.7 155.1 %reduce-scatter.41.cloned.1.call-start = ((), (), s32[]{:S(2)}) async-start(), calls=%async_computation.46 | async-start | bytes 3276800 | tf_op jit(solution)/shard_map/reduce_scatter | solution.py:269
  885.2 174.8 %reduce-scatter.43.cloned.1.call-start = ((), (), s32[]{:S(2)}) async-start(), calls=%async_computation.47 | async-start | bytes 3276800 | tf_op jit(solution)/shard_map/reduce_scatter | solution.py:270
  896.3 217.6 %reduce-scatter.57.cloned.1.call-start = ((), (), s32[]{:S(2)}) async-start(), calls=%async_computation.56 | async-start | bytes 3276800 | tf_op jit(solution)/shard_map/reduce_scatter | solution.py:269
  931.0 237.1 %reduce-scatter.59.cloned.1.call-start = ((), (), s32[]{:S(2)}) async-start(), calls=%async_computation.57 | async-start | bytes 3276800 | tf_op jit(solution)/shard_map/reduce_scatter | solution.py:270
  942.1 284.2 %reduce-scatter.53.cloned.1.call-start = ((), (), s32[]{:S(2)}) async-start(), calls=%async_computation.53 | async-start | bytes 1638400 | tf_op jit(solution)/shard_map/reduce_scatter | solution.py:301
  963.9 262.4 %reduce-scatter.45.cloned.1.call-start = ((), (), s32[]{:S(2)}) async-start(), calls=%async_computation.48 | async-start | bytes 1638400 | tf_op jit(solution)/shard_map/reduce_scatter | solution.py:301
  1065.9 188.5 %reduce-scatter.61.cloned.1.call-start = ((), (), s32[]{:S(2)}) async-start(), calls=%async_computation.58 | async-start | bytes 1638400 | tf_op jit(solution)/shard_map/reduce_scatter | solution.py:301
  1174.1 152.0 %reduce-scatter.69.cloned.1.call-start = ((), (), s32[]{:S(2)}) async-start(), calls=%async_computation.65 | async-start | bytes 2211840 | tf_op jit(solution)/shard_map/reduce_scatter | solution.py:315
  1180.6 216.2 %reduce-scatter.63.cloned.1.call-start = ((), (), s32[]{:S(2)}) async-start(), calls=%async_computation.62 | async-start | bytes 2211840 | tf_op jit(solution)/shard_map/reduce_scatter | solution.py:312
  1186.2 335.4 %reduce-scatter.73.cloned.1.call-start = ((), (), s32[]{:S(2)}) async-start(), calls=%async_computation.67 | async-start | bytes 7372800
  1205.7 441.2 %reduce-scatter.71.cloned.1.call-start = ((), (), s32[]{:S(2)}) async-start(), calls=%async_computation.66 | async-start | bytes 7372800 | tf_op jit(solution)/shard_map/reduce_scatter | solution.py:316
  1216.8 430.0 %all-reduce.3.cloned.1.call-start = ((), (), s32[]{:S(2)}) async-start(), calls=%async_computation.68 | async-start | bytes 188416 | tf_op jit(solution)/shard_map/psum | solution.py:332
  1257.8 459.9 %reduce-scatter.67.cloned.1.call-start = ((), (), s32[]{:S(2)}) async-start(), calls=%async_computation.64 | async-start | bytes 2211840 | tf_op jit(solution)/shard_map/reduce_scatter | solution.py:314
  1262.0 526.1 %reduce-scatter.65.cloned.1.call-start = ((), (), s32[]{:S(2)}) async-start(), calls=%async_computation.63 | async-start | bytes 2211840 | tf_op jit(solution)/shard_map/reduce_scatter | solution.py:313
  (206 other events, 4464.3 us)
Sparse Core Ops, SparseCore 0:
  13.4 20.8 all-gather.23
  36.5 18.1 all-gather.43
  56.8 18.1 all-gather.35
  76.4 39.3 all-gather.27
  120.7 42.6 all-gather.25
  164.8 45.2 all-gather.47
  211.7 31.6 all-gather.45
  244.9 31.6 all-gather.39
  278.2 31.6 all-gather.37
  312.2 33.6 reduce-scatter.26
  348.4 34.4 reduce-scatter.34
  385.3 34.4 reduce-scatter.30
  745.7 18.1 all-gather.53
  805.0 18.1 all-gather.51
  825.2 18.1 all-gather.55
  845.6 52.2 reduce-scatter.48
  900.0 51.7 reduce-scatter.50
  954.0 51.7 reduce-scatter.40
  1008.2 51.7 reduce-scatter.42
  1062.1 51.7 reduce-scatter.56
  1116.3 51.7 reduce-scatter.58
  1170.7 25.9 reduce-scatter.52
  1199.2 26.3 reduce-scatter.44
  1228.0 26.4 reduce-scatter.60
  1258.5 67.5 reduce-scatter.68
  1329.9 66.8 reduce-scatter.62
  1400.9 120.6 reduce-scatter.72
  1525.8 120.9 reduce-scatter.70
  1650.9 66.7 reduce-scatter.66
  1721.6 66.4 reduce-scatter.64
Sparse Core Ops, SparseCore 1:
  322.7 60.4 all-gather.31
  423.8 18.0 all-gather.29
  443.3 18.0 all-gather.57
  463.5 61.3 all-gather.33
  526.9 16.7 all-gather.49
  545.2 18.0 all-gather.61
  565.3 18.0 all-gather.41
  584.8 18.0 all-gather.59
  605.3 34.3 reduce-scatter.38
  642.2 34.4 reduce-scatter.54
  679.0 34.4 reduce-scatter.46
  716.0 26.3 reduce-scatter.32
  745.4 26.3 reduce-scatter.36
  774.3 26.3 reduce-scatter.28
  1257.9 138.5 all-reduce.2
